TPU v7x, 32 devices: a whole 2x2x4 slice. The times are simulated.
32 devices in a mesh: reg: 16 (over z, x, core), lev: 2 (over y).
Axes of the slice: x: 2, y: 2, z: 4, core: 2. Of those that a mesh axis runs over, the one named last changes fastest.
Arguments:
- state_now: bfloat16 [24, 1280, 2560], P(None, 'reg', 'lev'), may hold values from -6 to 6
- dep_cell: int32 [8, 1280, 2560], P(None, 'reg', 'lev'), may hold values from 0 to 63, as said below
- weight_code: int32 [8, 1280, 2560], P(None, 'reg', 'lev'), may hold values from 0 to 288, as said below
- wave_speed: float32 [8], replicated, may hold values from 0.05 to 5
Outputs:
- state_next: bfloat16 [24, 1280, 2560], P(None, 'reg', 'lev')
Inputs may be any that keep to these rules, and one draw needn't show every extreme that they name: `dep_cell`: 2 * 4 (a + 4) + b + 4 with whole numbers a and b from -4 to 3; both ends of that range occur for a and for b. `weight_code`: 17 a + b with whole numbers a and b from 0 to 16.
All inputs are finite; a program needn't handle non-finite values.
Results may differ from a plain program's by a relative error of at most 0.0084.
Values may be sent and summed in bfloat16 or wider, within the bound.
A program may use at most 64 MiB of HBM per device.

v0:
```python
import math
import jax
import jax.numpy as jnp
from jax import lax
from jax.sharding import PartitionSpec as P

NLAT = 1280
NLON = 2560
MX = 640
MY = 640
FIELDS = 3
HALO = 4


def padded_2(block, sides, width):
    for axis, dim in sides:
        count = lax.axis_size(axis)
        forward = [(i, i + 1) for i in range(count - 1)]
        forward.append((count - 1, 0))
        backward = [(target, source) for source, target in forward]
        low = lax.ppermute(
            lax.slice_in_dim(block, block.shape[dim] - width, None, axis=dim), axis, forward
        )
        high = lax.ppermute(lax.slice_in_dim(block, 0, width, axis=dim), axis, backward)
        block = jnp.concatenate([low, block, high], axis=dim)
    return block


def wave_table(length, modes, offset, amount):
    position = offset + lax.iota(jnp.int32, amount)
    wavenum = lax.iota(jnp.int32, 2 * modes) % modes
    product = position[:, None] * wavenum[None, :] % length
    angles = product.astype(jnp.float32) * (2.0 * math.pi / length)
    cosine_part = lax.iota(jnp.int32, 2 * modes) < modes
    return jnp.where(cosine_part[None, :], jnp.cos(angles), jnp.sin(angles)).astype(jnp.bfloat16)


def implicit_solve(spectral, xindex, speeds):
    wave_x = xindex % MX
    wave_y = lax.iota(jnp.int32, 2 * MY) % MY
    kx_term = 2.0 * math.pi / NLON * wave_x.astype(jnp.float32)
    ky_term = 2.0 * math.pi / NLAT * wave_y.astype(jnp.float32)
    laplace = kx_term[:, None] ** 2 + ky_term[None, :] ** 2
    inside = wave_x[:, None] * wave_x[:, None] + wave_y[None, :] * wave_y[None, :] < MX * MY
    weight_x = jnp.where(wave_x == 0, 1.0, 2.0)
    weight_y = jnp.where(wave_y == 0, 1.0, 2.0)
    factor = jnp.where(inside, weight_x[:, None] * weight_y[None, :], 0.0).astype(jnp.float32)
    speed_sq = speeds[:, None, None]
    vorticity = spectral[:, 0]
    divergence = spectral[:, 1]
    pressure = spectral[:, 2]
    div_new = (divergence + laplace * pressure) / (1.0 + speed_sq * laplace)
    pres_new = pressure - speed_sq * div_new
    stacked = jnp.stack([vorticity, div_new, pres_new], axis=1)
    return (stacked * factor[None, None]).astype(jnp.bfloat16)


def shift_weights(cell_code, code_index):
    shift_row = cell_code // (2 * HALO) - HALO
    shift_col = cell_code % (2 * HALO) - HALO
    weight_row = (code_index // 17).astype(jnp.float32) / 16.0
    weight_col = (code_index % 17).astype(jnp.float32) / 16.0
    row_weights = []
    col_weights = []
    for offset in range(-HALO, HALO + 1):
        row_weights.append(
            jnp.where(shift_row == offset, 1.0 - weight_row, 0.0)
            + jnp.where(shift_row + 1 == offset, weight_row, 0.0)
        )
        col_weights.append(
            jnp.where(shift_col == offset, 1.0 - weight_col, 0.0)
            + jnp.where(shift_col + 1 == offset, weight_col, 0.0)
        )
    return (row_weights, col_weights)


def interpolate_local(padded, row_weights, col_weights):
    levels, rows_pad, cols_pad = padded.shape
    rows_here = rows_pad - 2 * HALO
    cols_here = cols_pad - 2 * HALO
    blended = jnp.zeros((levels, rows_here, cols_here), jnp.float32)
    for row_step in range(2 * HALO + 1):
        inner = jnp.zeros((levels, rows_here, cols_here), jnp.float32)
        for col_step in range(2 * HALO + 1):
            window = padded[:, row_step : row_step + rows_here, col_step : col_step + cols_here]
            inner = inner + col_weights[col_step] * window.astype(jnp.float32)
        blended = blended + row_weights[row_step] * inner
    return blended.astype(jnp.bfloat16)


def per_device(state_now, dep_cell, weight_code, wave_speed):
    stacked, rows_here, cols_here = state_now.shape
    levels = stacked // FIELDS
    col_first = lax.axis_index("lev") * cols_here
    grouped = state_now.reshape(levels, FIELDS, rows_here, cols_here)
    row_weights, col_weights = shift_weights(dep_cell, weight_code)
    passes = []
    for which_field in range(FIELDS):
        padded = padded_2(grouped[:, which_field], (("reg", 1), ("lev", 2)), HALO)
        passes.append(interpolate_local(padded, row_weights, col_weights))
    upstream = jnp.stack(passes, axis=1).reshape(stacked, rows_here, cols_here)
    lon_table = wave_table(NLON, MX, 0, NLON)
    full_rows = lax.all_to_all(upstream, "lev", split_axis=0, concat_axis=2, tiled=True)
    lon_sum = jnp.einsum("krj,jc->krc", full_rows, lon_table, preferred_element_type=jnp.float32)
    lon_coef = (lon_sum / NLON).astype(jnp.bfloat16)
    lat_table = wave_table(NLAT, MY, 0, NLAT)
    spectral = (
        jnp.einsum(
            "klc,ly->kcy",
            lax.all_to_all(lon_coef, "reg", split_axis=2, concat_axis=1, tiled=True),
            lat_table,
            preferred_element_type=jnp.float32,
        )
        / NLAT
    )
    share = spectral.shape[1]
    xindex = lax.axis_index("reg") * share + lax.iota(jnp.int32, share)
    level_count = spectral.shape[0] // FIELDS
    speeds = lax.dynamic_slice_in_dim(
        wave_speed, lax.axis_index("lev") * level_count, level_count, 0
    )
    solved = implicit_solve(spectral.reshape(level_count, FIELDS, share, 2 * MY), xindex, speeds)
    solved = solved.reshape(level_count * FIELDS, share, 2 * MY)
    back_lat = jnp.einsum(
        "kcy,ly->kcl", solved, lat_table, preferred_element_type=jnp.float32
    ).astype(jnp.bfloat16)
    back_coef = lax.all_to_all(back_lat, "reg", split_axis=2, concat_axis=1, tiled=True)
    own_table = wave_table(NLON, MX, col_first, cols_here)
    return jnp.einsum(
        "kcr,jc->krj",
        lax.all_gather(back_coef, "lev", axis=0, tiled=True),
        own_table,
        preferred_element_type=jnp.float32,
    ).astype(jnp.bfloat16)


def solution(mesh):
    placed = (P(None, "reg", "lev"), P(None, "reg", "lev"), P(None, "reg", "lev"), P())
    return jax.shard_map(
        per_device, mesh=mesh, in_specs=placed, out_specs=P(None, "reg", "lev"), check_vma=False
    )
```

profile of v0, /device:TPU:0, one launch (start us, length us, event | category | flops | bytes accessed | tf_op | source)
XLA Modules:
  0.0 738.9 jit_solution(3293429734263387196)
XLA Ops:
  6.5 2.7 slice_bitcast_fusion.2
  9.3 0.0 copy-start.2
  9.3 0.1 fusion.90
  9.4 0.5 collective-permute-start
  9.9 5.0 collective-permute-start.1
  14.9 0.1 fusion.91
  15.0 0.1 collective-permute-start.4
  15.1 4.4 collective-permute-start.5
  19.5 0.1 fusion.92
  19.6 0.1 collective-permute-start.8
  19.6 4.4 collective-permute-start.9
  24.1 0.1 pad_maximum_fusion.19
  24.2 2.0 collective-permute-start.2
  26.2 0.1 collective-permute-start.3
  26.3 0.1 pad_maximum_fusion.16
  26.5 2.0 collective-permute-start.6
  28.5 0.1 collective-permute-start.7
  28.6 0.9 pad_maximum_fusion.13
  29.5 1.9 collective-permute-start.10
  31.4 0.4 collective-permute-done.2
  31.8 1.9 collective-permute-start.11
  33.7 1.9 collective-permute-done.3
  35.6 2.3 maximum_maximum_fusion
  37.9 0.0 copy-start
  38.0 1.5 collective-permute-done.6
  39.5 3.0 collective-permute-done.7
  42.5 2.3 maximum_maximum_fusion.1
  44.9 75.1 %fusion.69 = bf16[8,1,80,1280]{3,2,0,1:T(8,128)(2,1)} fusion(bf16[8,88,1284]{2,1,0:T(8,128)(2,1)S(1)} %get-tuple-element.12, bf16[8,4,1280]{2,1,0:T(4,128)(2,1)S(1)} %collective-permute-done.1, bf16[8,80,1280]{2,1,0:T(8,128)(2,1)} %copy-done.4, bf16[8,88,1284]{2,1,0:T(8,128)(2,1)S(1)} %get-tuple-element.11, ...), kind=kLoop, calls=%fused_computation.152 | loop fusion | flops 333414400 | bytes 127959040 | tf_op jit(solution)/shard_map/stack | solution.py:101
  120.0 76.8 %fusion.70 = bf16[8,1,80,1280]{3,2,0,1:T(8,128)(2,1)} fusion(bf16[8,88,1284]{2,1,0:T(8,128)(2,1)S(1)} %get-tuple-element.16, bf16[8,4,1280]{2,1,0:T(4,128)(2,1)} %copy-done.8, bf16[8,80,1280]{2,1,0:T(8,128)(2,1)} %copy-done.3, bf16[8,88,1284]{2,1,0:T(8,128)(2,1)S(1)} %get-tuple-element.15, bf16[8,4,1280]{2,1,0:T(4,128)(2,1)} %copy-done.5, ...), kind=kLoop, calls=%fused_computation.153 | loop fusion | flops 333414400 | bytes 127959040 | tf_op jit(solution)/shard_map/stack | solution.py:101
  196.8 0.0 copy-start.1
  196.9 4.3 maximum_maximum_fusion.2
  201.2 75.0 %fusion.71 = bf16[8,1,80,1280]{3,2,0,1:T(8,128)(2,1)} fusion(bf16[8,88,1284]{2,1,0:T(8,128)(2,1)S(1)} %get-tuple-element.20, bf16[8,4,1280]{2,1,0:T(4,128)(2,1)S(1)} %copy-done.7, bf16[8,80,1280]{2,1,0:T(8,128)(2,1)} %copy-done.2, bf16[8,88,1284]{2,1,0:T(8,128)(2,1)S(1)} %get-tuple-element.19, bf16[8,4,1280]{2,1,0:T(4,128)(2,1)S(1)} %collective-permute-done.8, ...), kind=kLoop, calls=%fused_computation.154 | loop fusion | flops 333414400 | bytes 127959040 | tf_op jit(solution)/shard_map/stack | solution.py:101
  276.2 2.9 pad_maximum_fusion
  279.1 2.6 copy.15
  281.7 6.3 all-to-all-start
  288.1 47.1 %all-to-all-done = bf16[24,80,1280]{2,1,0:T(8,128)(2,1)} async-done(((bf16[24,80,1280]{2,1,0:T(8,128)(2,1)}), bf16[24,80,1280]{2,1,0:T(8,128)(2,1)}, u32[]{:S(2)}, u32[]{:S(2)}) %all-to-all-start) | async-done | bytes 4915232 | tf_op jit(solution)/shard_map/all_to_all | solution.py:103
  335.1 2.8 copy.23
  338.0 58.4 %multiply_convert_fusion = bf16[12,80,1280]{2,1,0:T(8,128)(2,1)S(1)} fusion(bf16[12,80,2560]{2,1,0:T(8,128)(2,1)S(1)} %bitcast.85, s32[1280]{0:T(1024)S(1)} %add_select_fusion.7, pred[1280]{0:T(1024)(128)(4,1)S(1)} %iota_compare_fusion), kind=kOutput, calls=%fused_computation.36 | convolution fusion | flops 6329958400 | bytes 7379200 | tf_op jit(solution)/shard_map/krj,jc->krc/dot_general | solution.py:104
  396.4 5.9 copy.17
  402.3 9.9 %reshape.160 = bf16[16,2,38400]{2,1,0:T(2,128)(2,1)} reshape(bf16[1280,12,80]{2,1,0:T(8,128)(2,1)} %bitcast.79) | data formatting | bytes 4915200
  412.2 6.3 all-to-all-start.1
  418.5 0.0 all-gather.2.cloned.1.call-start
  418.5 0.1 dynamic_slice.3
  418.7 0.1 broadcast_add_fusion
  418.8 0.1 multiply_select_fusion
  418.9 46.9 %all-to-all-done.1 = bf16[16,2,38400]{2,1,0:T(2,128)(2,1)S(1)} async-done(((bf16[16,2,38400]{2,1,0:T(2,128)(2,1)}), bf16[16,2,38400]{2,1,0:T(2,128)(2,1)S(1)}, u32[]{:S(2)}, u32[]{:S(2)}) %all-to-all-start.1) | async-done | bytes 2457632 | tf_op jit(solution)/shard_map/all_to_all | solution.py:110
  465.8 9.3 %reshape.161 = bf16[1280,12,80]{2,1,0:T(8,128)(2,1)} reshape(bf16[16,2,38400]{2,1,0:T(2,128)(2,1)S(1)} %all-to-all-done.1) | data formatting | bytes 4915200
  475.1 6.9 copy.25
  482.1 6.1 all_to_all.46
  488.1 30.0 %convolution_multiply_fusion = f32[12,80,1280]{2,1,0:T(8,128)S(1)} fusion(bf16[12,1280,80]{1,2,0:T(8,128)(2,1)S(1)} %all_to_all.46, s32[1280]{0:T(1024)S(1)} %add_select_fusion.7, pred[1280]{0:T(1024)(128)(4,1)S(1)} %iota_compare_fusion), kind=kOutput, calls=%fused_computation.44 | convolution fusion | flops 3164979200 | bytes 7379200 | tf_op jit(solution)/shard_map/klc,ly->kcy/dot_general | solution.py:108
  518.2 0.5 multiply_subtract_fusion
  518.7 0.4 pad_maximum_fusion.1
  519.2 0.5 fusion.23
  519.6 30.3 %convolution_convert_fusion.1 = bf16[12,80,1280]{2,1,0:T(8,128)(2,1)S(1)} fusion(bf16[12,80,1280]{2,1,0:T(8,128)(2,1)S(1)} %fusion.23, s32[1280]{0:T(1024)S(1)} %add_select_fusion.7, pred[1280]{0:T(1024)(128)(4,1)S(1)} %iota_compare_fusion), kind=kOutput, calls=%fused_computation.46 | convolution fusion | flops 3164979200 | bytes 4921600 | tf_op jit(solution)/shard_map/kcy,ly->kcl/dot_general | solution.py:124
  549.9 5.7 copy.19
  555.6 8.8 %reshape.162 = bf16[16,2,38400]{2,1,0:T(2,128)(2,1)S(1)} reshape(bf16[1280,12,80]{2,1,0:T(8,128)(2,1)} %bitcast.80) | data formatting | bytes 4915200
  564.4 68.5 %all_to_all.54 = bf16[16,2,38400]{2,1,0:T(2,128)(2,1)} all-to-all(bf16[16,2,38400]{2,1,0:T(2,128)(2,1)S(1)} %reshape.162), channel_id=1, replica_groups=mesh['reg'=16,'lev'=2] {'reg'}, dimensions={0} | all-to-all | bytes 4915200 | tf_op jit(solution)/shard_map/all_to_all | solution.py:127
  633.0 10.7 %reshape.163 = bf16[1280,12,80]{2,1,0:T(8,128)(2,1)} reshape(bf16[16,2,38400]{2,1,0:T(2,128)(2,1)} %all_to_all.54) | data formatting | bytes 4915200
  643.7 6.9 copy.20
  650.6 7.1 all_to_all.50
  657.8 0.0 all-gather.2.cloned.1.call-update
  657.8 27.7 %fusion.109 = bf16[1280,1280,1]{1,0,2:T(8,128)(2,1)S(1)} fusion(s32[1280]{0:T(1024)S(1)} %iota_add_fusion, s32[1280]{0:T(1024)S(1)} %add_select_fusion.7, pred[1280]{0:T(1024)(128)(4,1)S(1)} %iota_compare_fusion), kind=kLoop, calls=%fused_computation.48.clone.clone.1 | loop fusion | flops 18022400 | bytes 3288320 | tf_op jit(solution)/shard_map/kcr,jc->krj/dot_general | solution.py:129
  685.5 36.1 %all-gather.2.cloned.1.call-done = bf16[24,1280,80]{1,2,0:T(8,128)(2,1)} async-done(((bf16[12,1280,80]{1,2,0:T(8,128)(2,1)}), bf16[24,1280,80]{1,2,0:T(8,128)(2,1)}) %all-gather.2.cloned.1.call-update) | async-done | bytes 4915216 | tf_op jit(solution)/shard_map/all_gather | solution.py:131
  721.7 9.9 %convolution_convert_fusion = bf16[24,80,1280]{2,1,0:T(8,128)(2,1)} fusion(bf16[24,1280,80]{1,2,0:T(8,128)(2,1)} %all-gather.2.cloned.1.call-done, bf16[1280,1280,1]{1,0,2:T(8,128)(2,1)S(1)} %fusion.109), kind=kOutput, calls=%fused_computation.31 | convolution fusion | flops 6293913600 | bytes 13107200 | tf_op jit(solution)/shard_map/kcr,jc->krj/dot_general | solution.py:129
  (33 shorter events, 0.1 us)
Async XLA Ops:
  9.3 20.2 %copy-start.2 = (bf16[8,80,1280]{2,1,0:T(8,128)(2,1)}, bf16[8,80,1280]{2,1,0:T(8,128)(2,1)S(1)}, u32[]{:S(2)}) copy-start(bf16[8,80,1280]{2,1,0:T(8,128)(2,1)S(1)} %get-tuple-element.9) | copy-start | bytes 4915204
  9.3 26.3 %copy-start.4 = (bf16[8,80,1280]{2,1,0:T(8,128)(2,1)}, bf16[8,80,1280]{2,1,0:T(8,128)(2,1)S(1)}, u32[]{:S(2)}) copy-start(bf16[8,80,1280]{2,1,0:T(8,128)(2,1)S(1)} %get-tuple-element.8) | copy-start | bytes 4915204
  9.3 33.2 %copy-start.3 = (bf16[8,80,1280]{2,1,0:T(8,128)(2,1)}, bf16[8,80,1280]{2,1,0:T(8,128)(2,1)S(1)}, u32[]{:S(2)}) copy-start(bf16[8,80,1280]{2,1,0:T(8,128)(2,1)S(1)} %get-tuple-element.10) | copy-start | bytes 4915204
  9.4 10.2 %collective-permute-start = (bf16[8,4,1280]{2,1,0:T(4,128)(2,1)S(1)}, bf16[8,4,1280]{2,1,0:T(4,128)(2,1)S(1)}, u32[]{:S(2)}, u32[]{:S(2)}) collective-permute-start(bf16[8,4,1280]{2,1,0:T(4,128)(2,1)S(1)} %get-tuple-element.23), channel_id=1, source_target_pairs={{0,2},{2,4},{4,6},{6,8},{8,10},{10,12},{12,14},{14,16},{16,18},{18... | collective-permute-start | bytes 245768 | tf_op jit(solution)/shard_map/ppermute | solution.py:21
  9.9 14.2 %collective-permute-start.1 = (bf16[8,4,1280]{2,1,0:T(4,128)(2,1)S(1)}, bf16[8,4,1280]{2,1,0:T(4,128)(2,1)S(1)}, u32[]{:S(2)}, u32[]{:S(2)}) collective-permute-start(bf16[8,4,1280]{2,1,0:T(4,128)(2,1)S(1)} %get-tuple-element.24), channel_id=1, source_target_pairs={{2,0},{4,2},{6,4},{8,6},{10,8},{12,10},{14,12},{16,14},{18,16},{20... | collective-permute-start | bytes 245768 | tf_op jit(solution)/shard_map/ppermute | solution.py:24
  15.0 11.2 %collective-permute-start.4 = (bf16[8,4,1280]{2,1,0:T(4,128)(2,1)S(1)}, bf16[8,4,1280]{2,1,0:T(4,128)(2,1)S(1)}, u32[]{:S(2)}, u32[]{:S(2)}) collective-permute-start(bf16[8,4,1280]{2,1,0:T(4,128)(2,1)S(1)} %get-tuple-element.25), channel_id=1, source_target_pairs={{0,2},{2,4},{4,6},{6,8},{8,10},{10,12},{12,14},{14,16},{16,18},{18... | collective-permute-start | bytes 245768 | tf_op jit(solution)/shard_map/ppermute | solution.py:21
  15.1 11.3 %collective-permute-start.5 = (bf16[8,4,1280]{2,1,0:T(4,128)(2,1)S(1)}, bf16[8,4,1280]{2,1,0:T(4,128)(2,1)S(1)}, u32[]{:S(2)}, u32[]{:S(2)}) collective-permute-start(bf16[8,4,1280]{2,1,0:T(4,128)(2,1)S(1)} %get-tuple-element.26), channel_id=1, source_target_pairs={{2,0},{4,2},{6,4},{8,6},{10,8},{12,10},{14,12},{16,14},{18,16},{20... | collective-permute-start | bytes 245768 | tf_op jit(solution)/shard_map/ppermute | solution.py:24
  19.6 8.9 %collective-permute-start.8 = (bf16[8,4,1280]{2,1,0:T(4,128)(2,1)S(1)}, bf16[8,4,1280]{2,1,0:T(4,128)(2,1)S(1)}, u32[]{:S(2)}, u32[]{:S(2)}) collective-permute-start(bf16[8,4,1280]{2,1,0:T(4,128)(2,1)S(1)} %get-tuple-element.27), channel_id=1, source_target_pairs={{0,2},{2,4},{4,6},{6,8},{8,10},{10,12},{12,14},{14,16},{16,18},{18... | collective-permute-start | bytes 245768 | tf_op jit(solution)/shard_map/ppermute | solution.py:21
  19.6 8.9 %collective-permute-start.9 = (bf16[8,4,1280]{2,1,0:T(4,128)(2,1)S(1)}, bf16[8,4,1280]{2,1,0:T(4,128)(2,1)S(1)}, u32[]{:S(2)}, u32[]{:S(2)}) collective-permute-start(bf16[8,4,1280]{2,1,0:T(4,128)(2,1)S(1)} %get-tuple-element.28), channel_id=1, source_target_pairs={{2,0},{4,2},{6,4},{8,6},{10,8},{12,10},{14,12},{16,14},{18,16},{20... | collective-permute-start | bytes 245768 | tf_op jit(solution)/shard_map/ppermute | solution.py:24
  24.2 7.6 %collective-permute-start.2 = (bf16[8,88,4]{2,1,0:T(8,128)(2,1)S(1)}, bf16[8,88,4]{2,1,0:T(8,128)(2,1)S(1)}, u32[]{:S(2)}, u32[]{:S(2)}) collective-permute-start(bf16[8,88,4]{2,1,0:T(8,128)(2,1)S(1)} %get-tuple-element.13), channel_id=1, source_target_pairs={{0,1},{1,0},{2,3},{3,2},{4,5},{5,4},{6,7},{7,6},{8,9},{9,8},{10,11... | collective-permute-start | bytes 16904 | tf_op jit(solution)/shard_map/ppermute | solution.py:21
  26.2 16.3 %copy-start.5 = (bf16[8,4,1280]{2,1,0:T(4,128)(2,1)}, bf16[8,4,1280]{2,1,0:T(4,128)(2,1)S(1)}, u32[]{:S(2)}) copy-start(bf16[8,4,1280]{2,1,0:T(4,128)(2,1)S(1)} %collective-permute-done.4) | copy-start | bytes 245764
  26.2 9.4 %collective-permute-start.3 = (bf16[8,88,4]{2,1,0:T(8,128)(2,1)S(1)}, bf16[8,88,4]{2,1,0:T(8,128)(2,1)S(1)}, u32[]{:S(2)}, u32[]{:S(2)}) collective-permute-start(bf16[8,88,4]{2,1,0:T(8,128)(2,1)S(1)} %get-tuple-element.14), channel_id=1, source_target_pairs={{1,0},{0,1},{3,2},{2,3},{5,4},{4,5},{7,6},{6,7},{9,8},{8,9},{11,10... | collective-permute-start | bytes 16904 | tf_op jit(solution)/shard_map/ppermute | solution.py:24
  26.3 16.2 %copy-start.8 = (bf16[8,4,1280]{2,1,0:T(4,128)(2,1)}, bf16[8,4,1280]{2,1,0:T(4,128)(2,1)S(1)}, u32[]{:S(2)}) copy-start(bf16[8,4,1280]{2,1,0:T(4,128)(2,1)S(1)} %collective-permute-done.5) | copy-start | bytes 245764
  26.5 13.0 %collective-permute-start.6 = (bf16[8,88,4]{2,1,0:T(8,128)(2,1)S(1)}, bf16[8,88,4]{2,1,0:T(8,128)(2,1)S(1)}, u32[]{:S(2)}, u32[]{:S(2)}) collective-permute-start(bf16[8,88,4]{2,1,0:T(8,128)(2,1)S(1)} %get-tuple-element.17), channel_id=1, source_target_pairs={{0,1},{1,0},{2,3},{3,2},{4,5},{5,4},{6,7},{7,6},{8,9},{9,8},{10,11... | collective-permute-start | bytes 16904 | tf_op jit(solution)/shard_map/ppermute | solution.py:21
  28.5 14.1 %collective-permute-start.7 = (bf16[8,88,4]{2,1,0:T(8,128)(2,1)S(1)}, bf16[8,88,4]{2,1,0:T(8,128)(2,1)S(1)}, u32[]{:S(2)}, u32[]{:S(2)}) collective-permute-start(bf16[8,88,4]{2,1,0:T(8,128)(2,1)S(1)} %get-tuple-element.18), channel_id=1, source_target_pairs={{1,0},{0,1},{3,2},{2,3},{5,4},{4,5},{7,6},{6,7},{9,8},{8,9},{11,10... | collective-permute-start | bytes 16904 | tf_op jit(solution)/shard_map/ppermute | solution.py:24
  28.6 5.1 copy-start.6
  29.5 167.4 %collective-permute-start.10 = (bf16[8,88,4]{2,1,0:T(8,128)(2,1)}, bf16[8,88,4]{2,1,0:T(8,128)(2,1)}, u32[]{:S(2)}, u32[]{:S(2)}) collective-permute-start(bf16[8,88,4]{2,1,0:T(8,128)(2,1)} %get-tuple-element.21), channel_id=1, source_target_pairs={{0,1},{1,0},{2,3},{3,2},{4,5},{5,4},{6,7},{7,6},{8,9},{9,8},{10,11... | collective-permute-start | bytes 16904 | tf_op jit(solution)/shard_map/ppermute | solution.py:21
  31.8 165.1 %collective-permute-start.11 = (bf16[8,88,4]{2,1,0:T(8,128)(2,1)}, bf16[8,88,4]{2,1,0:T(8,128)(2,1)}, u32[]{:S(2)}, u32[]{:S(2)}) collective-permute-start(bf16[8,88,4]{2,1,0:T(8,128)(2,1)} %get-tuple-element.22), channel_id=1, source_target_pairs={{1,0},{0,1},{3,2},{2,3},{5,4},{4,5},{7,6},{6,7},{9,8},{8,9},{11,10... | collective-permute-start | bytes 16904 | tf_op jit(solution)/shard_map/ppermute | solution.py:24
  37.9 6.9 copy-start
  120.0 76.9 %copy-start.7 = (bf16[8,4,1280]{2,1,0:T(4,128)(2,1)S(1)}, bf16[8,4,1280]{2,1,0:T(4,128)(2,1)}, u32[]{:S(2)}) copy-start(bf16[8,4,1280]{2,1,0:T(4,128)(2,1)} %copy-done.6) | copy-start | bytes 245764
  196.8 4.3 copy-start.1
  281.7 53.4 %all-to-all-start = ((bf16[24,80,1280]{2,1,0:T(8,128)(2,1)}), bf16[24,80,1280]{2,1,0:T(8,128)(2,1)}, u32[]{:S(2)}, u32[]{:S(2)}) async-start(bf16[24,80,1280]{2,1,0:T(8,128)(2,1)} %bitcast.81), calls=%async_computation | async-start | bytes 9830400 | tf_op jit(solution)/shard_map/all_to_all | solution.py:103
  412.2 6.3 copy-start.9
  412.2 53.7 %all-to-all-start.1 = ((bf16[16,2,38400]{2,1,0:T(2,128)(2,1)}), bf16[16,2,38400]{2,1,0:T(2,128)(2,1)S(1)}, u32[]{:S(2)}, u32[]{:S(2)}) async-start(bf16[16,2,38400]{2,1,0:T(2,128)(2,1)} %reshape.160), calls=%async_computation.1 | async-start | bytes 4915200 | tf_op jit(solution)/shard_map/all_to_all | solution.py:110
  418.5 303.2 %all-gather.2.cloned.1.call-start = ((), (), s32[]{:S(2)}) async-start(), calls=%async_computation.3 | async-start | bytes 7372800 | tf_op jit(solution)/shard_map/all_gather | solution.py:131
Sparse Core Ops, SparseCore 0:
  657.9 63.7 all-gather.1
where the time goes:
time: 747 us; the launch traced here: 739 us
  other arithmetic  269 us (36%)
  waiting for transfers between devices  137 us (18%)
  matrix products  129 us (17%)
  local copies, waits for them, and re-layouts  85.9 us (11%)
  blocking collectives  68.5 us (9%)
  starting transfers between devices  35.2 us (5%)
  between operations  14.2 us (2%)
    another operation x4, other arithmetic, per_device(): upstream = jnp.stack(passes, axis=1).reshape(stacked, rows_here, cols_here)  230 us
    all_to_all x1, blocking collectives, per_device(): lax.all_to_all(back_lat, 'reg', split_axis=2, concat_axis=1, tiled=True)  68.5 us
    dot_general x1, matrix products, per_device(): jnp.einsum('krj,jc->krc', full_rows, lon_table, preferred_element_type=jn...  58.4 us
    all_to_all x1, waiting for transfers between devices, per_device(): lax.all_to_all(upstream, 'lev', split_axis=0, concat_axis=2, tiled=True)  47.1 us
    all_to_all x1, waiting for transfers between devices, per_device(): lax.all_to_all(lon_coef, 'reg', split_axis=2, concat_axis=1, tiled=True)  46.9 us
    unnamed x24, local copies, waits for them, and re-layouts  38.7 us
    all_gather x1, waiting for transfers between devices, per_device(): lax.all_gather(back_coef, 'lev', axis=0, tiled=True)  36.1 us
    dot_general x1, matrix products, per_device(): jnp.einsum('kcy,ly->kcl', solved, lat_table, preferred_element_type=jnp.f...  30.3 us
  transfers between devices with their start and end apart: 15, of which 7 were waited for; matrix products, arithmetic and copies ran while one was open for 25% of the time, Pallas kernels for 0%

commit v1 on v0

--- a/solution.py
+++ b/solution.py
@@ -10,6 +10,18 @@
 MY = 640
 FIELDS = 3
 HALO = 4
+
+
+def gather_by_bits(x, axis, dim):
+    ways, here = (lax.axis_size(axis), lax.axis_index(axis))
+    grown, reach = (x, 1)
+    while reach < ways:
+        theirs = lax.ppermute(grown, axis, [(d, d ^ reach) for d in range(ways)])
+        mine_first = jnp.concatenate([grown, theirs], axis=dim)
+        theirs_first = jnp.concatenate([theirs, grown], axis=dim)
+        grown = jnp.where(here & reach == 0, mine_first, theirs_first)
+        reach = 2 * reach
+    return grown
 
 
 def padded_2(block, sides, width):
@@ -128,7 +140,7 @@
     own_table = wave_table(NLON, MX, col_first, cols_here)
     return jnp.einsum(
         "kcr,jc->krj",
-        lax.all_gather(back_coef, "lev", axis=0, tiled=True),
+        gather_by_bits(back_coef, "lev", 0),
         own_table,
         preferred_element_type=jnp.float32,
     ).astype(jnp.bfloat16)

time: 747 us -> 725 us (0.971)
  between operations: 14.2 us -> 0.81 us
  waiting for transfers between devices: 137 us -> 129 us
    all_gather x1 -> x0, waiting for transfers between devices: 36.1 us -> none  [per_device(): lax.all_gather(back_coef, 'lev', axis=0, tiled=True)]
    ppermute x0 -> x1, waiting for transfers between devices: none -> 28.4 us  [gather_by_bits(): theirs = lax.ppermute(grown, axis, [(d, d ^ reach) for d in range(ways)])]
  transfers between devices with their start and end apart: 15 -> 15, of which waited for: 7 -> 7; matrix products, arithmetic and copies ran while one was open for 25% -> 26% of each run, Pallas kernels for 0% -> 0%
where the time goes in v1:
time: 725 us; the launch traced here: 717 us
  other arithmetic  269 us (37%)
  waiting for transfers between devices  129 us (18%)
  matrix products  129 us (18%)
  local copies, waits for them, and re-layouts  84.8 us (12%)
  blocking collectives  68.5 us (9%)
  starting transfers between devices  35.2 us (5%)
    another operation x4, other arithmetic, per_device(): upstream = jnp.stack(passes, axis=1).reshape(stacked, rows_here, cols_here)  229 us
    all_to_all x1, blocking collectives, per_device(): lax.all_to_all(back_lat, 'reg', split_axis=2, concat_axis=1, tiled=True)  68.5 us
    dot_general x1, matrix products, per_device(): jnp.einsum('krj,jc->krc', full_rows, lon_table, preferred_element_type=jn...  58.4 us
    all_to_all x1, waiting for transfers between devices, per_device(): lax.all_to_all(upstream, 'lev', split_axis=0, concat_axis=2, tiled=True)  47.1 us
    all_to_all x1, waiting for transfers between devices, per_device(): lax.all_to_all(lon_coef, 'reg', split_axis=2, concat_axis=1, tiled=True)  47 us
    unnamed x24, local copies, waits for them, and re-layouts  38.7 us
    dot_general x1, matrix products, per_device(): jnp.einsum('kcy,ly->kcl', solved, lat_table, preferred_element_type=jnp.f...  30.3 us
    dot_general x1, matrix products, per_device(): jnp.einsum('klc,ly->kcy', lax.all_to_all(lon_coef, 'reg', split_axis=2, c...  30 us
  transfers between devices with their start and end apart: 15, of which 7 were waited for; matrix products, arithmetic and copies ran while one was open for 26% of the time, Pallas kernels for 0%

profile of v1, /device:TPU:0, one launch (start us, length us, event | category | flops | bytes accessed | tf_op | source)
XLA Modules:
  0.0 716.6 jit_solution(4747754501743831405)
XLA Ops:
  0.0 2.7 slice_bitcast_fusion.2
  2.7 0.0 copy-start.2
  2.8 0.1 fusion.97
  2.9 0.5 collective-permute-start
  3.4 5.0 collective-permute-start.1
  8.4 0.1 fusion.98
  8.5 0.1 collective-permute-start.4
  8.5 4.4 collective-permute-start.5
  13.0 0.1 fusion.99
  13.0 0.1 collective-permute-start.8
  13.1 4.4 collective-permute-start.9
  17.5 0.0 collective-permute-done.1
  17.5 0.1 pad_maximum_fusion.19
  17.7 2.0 collective-permute-start.2
  19.7 0.1 collective-permute-start.3
  19.8 0.1 pad_maximum_fusion.16
  19.9 2.0 collective-permute-start.6
  21.9 0.1 collective-permute-start.7
  22.0 0.9 pad_maximum_fusion.13
  22.9 1.9 collective-permute-start.10
  24.8 0.4 collective-permute-done.2
  25.2 1.9 collective-permute-start.11
  27.2 1.9 collective-permute-done.3
  29.1 2.3 maximum_maximum_fusion
  31.4 0.0 copy-start
  31.4 1.5 collective-permute-done.6
  33.0 3.0 collective-permute-done.7
  36.0 2.3 maximum_maximum_fusion.1
  38.3 75.1 %fusion.75 = bf16[8,1,80,1280]{3,2,0,1:T(8,128)(2,1)} fusion(bf16[8,88,1284]{2,1,0:T(8,128)(2,1)S(1)} %get-tuple-element.12, bf16[8,4,1280]{2,1,0:T(4,128)(2,1)S(1)} %collective-permute-done.1, bf16[8,80,1280]{2,1,0:T(8,128)(2,1)} %copy-done.4, bf16[8,88,1284]{2,1,0:T(8,128)(2,1)S(1)} %get-tuple-element.11, ...), kind=kLoop, calls=%fused_computation.159 | loop fusion | flops 333414400 | bytes 127959040 | tf_op jit(solution)/shard_map/stack | solution.py:113
  113.5 76.1 %fusion.76 = bf16[8,1,80,1280]{3,2,0,1:T(8,128)(2,1)} fusion(bf16[8,88,1284]{2,1,0:T(8,128)(2,1)S(1)} %get-tuple-element.16, bf16[8,4,1280]{2,1,0:T(4,128)(2,1)} %copy-done.8, bf16[8,80,1280]{2,1,0:T(8,128)(2,1)} %copy-done.3, bf16[8,88,1284]{2,1,0:T(8,128)(2,1)S(1)} %get-tuple-element.15, bf16[8,4,1280]{2,1,0:T(4,128)(2,1)} %copy-done.5, ...), kind=kLoop, calls=%fused_computation.160 | loop fusion | flops 333414400 | bytes 127959040 | tf_op jit(solution)/shard_map/stack | solution.py:113
  189.6 0.0 copy-start.1
  189.6 4.3 maximum_maximum_fusion.2
  193.9 75.0 %fusion.77 = bf16[8,1,80,1280]{3,2,0,1:T(8,128)(2,1)} fusion(bf16[8,88,1284]{2,1,0:T(8,128)(2,1)S(1)} %get-tuple-element.20, bf16[8,4,1280]{2,1,0:T(4,128)(2,1)S(1)} %copy-done.7, bf16[8,80,1280]{2,1,0:T(8,128)(2,1)} %copy-done.2, bf16[8,88,1284]{2,1,0:T(8,128)(2,1)S(1)} %get-tuple-element.19, bf16[8,4,1280]{2,1,0:T(4,128)(2,1)S(1)} %collective-permute-done.8, ...), kind=kLoop, calls=%fused_computation.161 | loop fusion | flops 333414400 | bytes 127959040 | tf_op jit(solution)/shard_map/stack | solution.py:113
  269.0 2.9 pad_maximum_fusion
  271.9 2.6 copy.15
  274.5 6.3 all-to-all-start
  280.8 47.1 %all-to-all-done = bf16[24,80,1280]{2,1,0:T(8,128)(2,1)} async-done(((bf16[24,80,1280]{2,1,0:T(8,128)(2,1)}), bf16[24,80,1280]{2,1,0:T(8,128)(2,1)}, u32[]{:S(2)}, u32[]{:S(2)}) %all-to-all-start) | async-done | bytes 4915232 | tf_op jit(solution)/shard_map/all_to_all | solution.py:115
  327.9 2.8 copy.23
  330.8 58.4 %multiply_convert_fusion = bf16[12,80,1280]{2,1,0:T(8,128)(2,1)S(1)} fusion(bf16[12,80,2560]{2,1,0:T(8,128)(2,1)S(1)} %bitcast.84, s32[1280]{0:T(1024)S(1)} %add_select_fusion.7, pred[1280]{0:T(1024)(128)(4,1)S(1)} %iota_compare_fusion), kind=kOutput, calls=%fused_computation.42 | convolution fusion | flops 6329958400 | bytes 7379200 | tf_op jit(solution)/shard_map/krj,jc->krc/dot_general | solution.py:116
  389.2 5.9 copy.17
  395.1 9.9 %reshape.160 = bf16[16,2,38400]{2,1,0:T(2,128)(2,1)} reshape(bf16[1280,12,80]{2,1,0:T(8,128)(2,1)} %bitcast.78) | data formatting | bytes 4915200
  405.0 6.3 all-to-all-start.1
  411.3 0.1 dynamic_slice.3
  411.4 0.1 broadcast_add_fusion
  411.5 0.1 multiply_select_fusion
  411.7 47.0 %all-to-all-done.1 = bf16[16,2,38400]{2,1,0:T(2,128)(2,1)S(1)} async-done(((bf16[16,2,38400]{2,1,0:T(2,128)(2,1)}), bf16[16,2,38400]{2,1,0:T(2,128)(2,1)S(1)}, u32[]{:S(2)}, u32[]{:S(2)}) %all-to-all-start.1) | async-done | bytes 2457632 | tf_op jit(solution)/shard_map/all_to_all | solution.py:122
  458.6 9.3 %reshape.161 = bf16[1280,12,80]{2,1,0:T(8,128)(2,1)} reshape(bf16[16,2,38400]{2,1,0:T(2,128)(2,1)S(1)} %all-to-all-done.1) | data formatting | bytes 4915200
  467.9 6.9 copy.25
  474.8 6.1 all_to_all.46
  480.9 30.0 %convolution_multiply_fusion = f32[12,80,1280]{2,1,0:T(8,128)S(1)} fusion(bf16[12,1280,80]{1,2,0:T(8,128)(2,1)S(1)} %all_to_all.46, s32[1280]{0:T(1024)S(1)} %add_select_fusion.7, pred[1280]{0:T(1024)(128)(4,1)S(1)} %iota_compare_fusion), kind=kOutput, calls=%fused_computation.51 | convolution fusion | flops 3164979200 | bytes 7379200 | tf_op jit(solution)/shard_map/klc,ly->kcy/dot_general | solution.py:120
  511.0 0.5 multiply_subtract_fusion
  511.5 0.4 pad_maximum_fusion.1
  511.9 0.5 fusion.28
  512.4 30.3 %convolution_convert_fusion.1 = bf16[12,80,1280]{2,1,0:T(8,128)(2,1)S(1)} fusion(bf16[12,80,1280]{2,1,0:T(8,128)(2,1)S(1)} %fusion.28, s32[1280]{0:T(1024)S(1)} %add_select_fusion.7, pred[1280]{0:T(1024)(128)(4,1)S(1)} %iota_compare_fusion), kind=kOutput, calls=%fused_computation.53 | convolution fusion | flops 3164979200 | bytes 4921600 | tf_op jit(solution)/shard_map/kcy,ly->kcl/dot_general | solution.py:136
  542.7 5.7 copy.19
  548.4 8.8 %reshape.162 = bf16[16,2,38400]{2,1,0:T(2,128)(2,1)S(1)} reshape(bf16[1280,12,80]{2,1,0:T(8,128)(2,1)} %bitcast.79) | data formatting | bytes 4915200
  557.2 68.5 %all_to_all.54 = bf16[16,2,38400]{2,1,0:T(2,128)(2,1)} all-to-all(bf16[16,2,38400]{2,1,0:T(2,128)(2,1)S(1)} %reshape.162), channel_id=1, replica_groups=mesh['reg'=16,'lev'=2] {'reg'}, dimensions={0} | all-to-all | bytes 4915200 | tf_op jit(solution)/shard_map/all_to_all | solution.py:139
  625.7 10.7 %reshape.163 = bf16[1280,12,80]{2,1,0:T(8,128)(2,1)} reshape(bf16[16,2,38400]{2,1,0:T(2,128)(2,1)} %all_to_all.54) | data formatting | bytes 4915200
  636.5 6.9 copy.20
  643.4 6.1 all_to_all.50
  649.5 0.1 collective-permute-start.12
  649.6 27.7 %fusion.115 = bf16[1280,1280,1]{1,0,2:T(8,128)(2,1)S(1)} fusion(s32[1280]{0:T(1024)S(1)} %iota_add_fusion, s32[1280]{0:T(1024)S(1)} %add_select_fusion.7, pred[1280]{0:T(1024)(128)(4,1)S(1)} %iota_compare_fusion), kind=kLoop, calls=%fused_computation.55.clone.clone.2 | loop fusion | flops 18022400 | bytes 3288320 | tf_op jit(solution)/shard_map/kcr,jc->krj/dot_general | solution.py:141
  677.3 28.4 %collective-permute-done.12 = bf16[12,1280,80]{1,2,0:T(8,128)(2,1)} collective-permute-done((bf16[12,1280,80]{1,2,0:T(8,128)(2,1)S(1)}, bf16[12,1280,80]{1,2,0:T(8,128)(2,1)}, u32[]{:S(2)}, u32[]{:S(2)}) %collective-permute-start.12) | collective-permute-done | bytes 2457632 | tf_op jit(solution)/shard_map/ppermute | solution.py:19
  705.7 10.5 %convolution_convert_fusion = bf16[24,80,1280]{2,1,0:T(8,128)(2,1)} fusion(bf16[12,1280,80]{1,2,0:T(8,128)(2,1)} %collective-permute-done.12, bf16[12,1280,80]{1,2,0:T(8,128)(2,1)S(1)} %all_to_all.50, pred[]{:T(512)S(6)} %eq.142, bf16[1280,1280,1]{1,0,2:T(8,128)(2,1)S(1)} %fusion.115), kind=kOutput, calls=%fused_computation.31 | convolution fusion | flops 6301286400 | bytes 13107201 | tf_op jit(solution)/shard_map/kcr,jc->krj/dot_general | solution.py:141
  (32 shorter events, 0.1 us)
Async XLA Ops:
  2.7 20.2 %copy-start.2 = (bf16[8,80,1280]{2,1,0:T(8,128)(2,1)}, bf16[8,80,1280]{2,1,0:T(8,128)(2,1)S(1)}, u32[]{:S(2)}) copy-start(bf16[8,80,1280]{2,1,0:T(8,128)(2,1)S(1)} %get-tuple-element.9) | copy-start | bytes 4915204
  2.8 26.3 %copy-start.4 = (bf16[8,80,1280]{2,1,0:T(8,128)(2,1)}, bf16[8,80,1280]{2,1,0:T(8,128)(2,1)S(1)}, u32[]{:S(2)}) copy-start(bf16[8,80,1280]{2,1,0:T(8,128)(2,1)S(1)} %get-tuple-element.8) | copy-start | bytes 4915204
  2.8 33.2 %copy-start.3 = (bf16[8,80,1280]{2,1,0:T(8,128)(2,1)}, bf16[8,80,1280]{2,1,0:T(8,128)(2,1)S(1)}, u32[]{:S(2)}) copy-start(bf16[8,80,1280]{2,1,0:T(8,128)(2,1)S(1)} %get-tuple-element.10) | copy-start | bytes 4915204
  2.9 10.2 %collective-permute-start = (bf16[8,4,1280]{2,1,0:T(4,128)(2,1)S(1)}, bf16[8,4,1280]{2,1,0:T(4,128)(2,1)S(1)}, u32[]{:S(2)}, u32[]{:S(2)}) collective-permute-start(bf16[8,4,1280]{2,1,0:T(4,128)(2,1)S(1)} %get-tuple-element.23), channel_id=1, source_target_pairs={{0,2},{2,4},{4,6},{6,8},{8,10},{10,12},{12,14},{14,16},{16,18},{18... | collective-permute-start | bytes 245768 | tf_op jit(solution)/shard_map/ppermute | solution.py:33
  3.4 14.2 %collective-permute-start.1 = (bf16[8,4,1280]{2,1,0:T(4,128)(2,1)S(1)}, bf16[8,4,1280]{2,1,0:T(4,128)(2,1)S(1)}, u32[]{:S(2)}, u32[]{:S(2)}) collective-permute-start(bf16[8,4,1280]{2,1,0:T(4,128)(2,1)S(1)} %get-tuple-element.24), channel_id=1, source_target_pairs={{2,0},{4,2},{6,4},{8,6},{10,8},{12,10},{14,12},{16,14},{18,16},{20... | collective-permute-start | bytes 245768 | tf_op jit(solution)/shard_map/ppermute | solution.py:36
  8.5 11.2 %collective-permute-start.4 = (bf16[8,4,1280]{2,1,0:T(4,128)(2,1)S(1)}, bf16[8,4,1280]{2,1,0:T(4,128)(2,1)S(1)}, u32[]{:S(2)}, u32[]{:S(2)}) collective-permute-start(bf16[8,4,1280]{2,1,0:T(4,128)(2,1)S(1)} %get-tuple-element.25), channel_id=1, source_target_pairs={{0,2},{2,4},{4,6},{6,8},{8,10},{10,12},{12,14},{14,16},{16,18},{18... | collective-permute-start | bytes 245768 | tf_op jit(solution)/shard_map/ppermute | solution.py:33
  8.5 11.3 %collective-permute-start.5 = (bf16[8,4,1280]{2,1,0:T(4,128)(2,1)S(1)}, bf16[8,4,1280]{2,1,0:T(4,128)(2,1)S(1)}, u32[]{:S(2)}, u32[]{:S(2)}) collective-permute-start(bf16[8,4,1280]{2,1,0:T(4,128)(2,1)S(1)} %get-tuple-element.26), channel_id=1, source_target_pairs={{2,0},{4,2},{6,4},{8,6},{10,8},{12,10},{14,12},{16,14},{18,16},{20... | collective-permute-start | bytes 245768 | tf_op jit(solution)/shard_map/ppermute | solution.py:36
  13.0 8.9 %collective-permute-start.8 = (bf16[8,4,1280]{2,1,0:T(4,128)(2,1)S(1)}, bf16[8,4,1280]{2,1,0:T(4,128)(2,1)S(1)}, u32[]{:S(2)}, u32[]{:S(2)}) collective-permute-start(bf16[8,4,1280]{2,1,0:T(4,128)(2,1)S(1)} %get-tuple-element.27), channel_id=1, source_target_pairs={{0,2},{2,4},{4,6},{6,8},{8,10},{10,12},{12,14},{14,16},{16,18},{18... | collective-permute-start | bytes 245768 | tf_op jit(solution)/shard_map/ppermute | solution.py:33
  13.1 8.9 %collective-permute-start.9 = (bf16[8,4,1280]{2,1,0:T(4,128)(2,1)S(1)}, bf16[8,4,1280]{2,1,0:T(4,128)(2,1)S(1)}, u32[]{:S(2)}, u32[]{:S(2)}) collective-permute-start(bf16[8,4,1280]{2,1,0:T(4,128)(2,1)S(1)} %get-tuple-element.28), channel_id=1, source_target_pairs={{2,0},{4,2},{6,4},{8,6},{10,8},{12,10},{14,12},{16,14},{18,16},{20... | collective-permute-start | bytes 245768 | tf_op jit(solution)/shard_map/ppermute | solution.py:36
  17.7 7.6 %collective-permute-start.2 = (bf16[8,88,4]{2,1,0:T(8,128)(2,1)S(1)}, bf16[8,88,4]{2,1,0:T(8,128)(2,1)S(1)}, u32[]{:S(2)}, u32[]{:S(2)}) collective-permute-start(bf16[8,88,4]{2,1,0:T(8,128)(2,1)S(1)} %get-tuple-element.13), channel_id=1, source_target_pairs={{0,1},{1,0},{2,3},{3,2},{4,5},{5,4},{6,7},{7,6},{8,9},{9,8},{10,11... | collective-permute-start | bytes 16904 | tf_op jit(solution)/shard_map/ppermute | solution.py:33
  19.7 16.3 %copy-start.5 = (bf16[8,4,1280]{2,1,0:T(4,128)(2,1)}, bf16[8,4,1280]{2,1,0:T(4,128)(2,1)S(1)}, u32[]{:S(2)}) copy-start(bf16[8,4,1280]{2,1,0:T(4,128)(2,1)S(1)} %collective-permute-done.4) | copy-start | bytes 245764
  19.7 9.4 %collective-permute-start.3 = (bf16[8,88,4]{2,1,0:T(8,128)(2,1)S(1)}, bf16[8,88,4]{2,1,0:T(8,128)(2,1)S(1)}, u32[]{:S(2)}, u32[]{:S(2)}) collective-permute-start(bf16[8,88,4]{2,1,0:T(8,128)(2,1)S(1)} %get-tuple-element.14), channel_id=1, source_target_pairs={{1,0},{0,1},{3,2},{2,3},{5,4},{4,5},{7,6},{6,7},{9,8},{8,9},{11,10... | collective-permute-start | bytes 16904 | tf_op jit(solution)/shard_map/ppermute | solution.py:36
  19.8 16.2 %copy-start.8 = (bf16[8,4,1280]{2,1,0:T(4,128)(2,1)}, bf16[8,4,1280]{2,1,0:T(4,128)(2,1)S(1)}, u32[]{:S(2)}) copy-start(bf16[8,4,1280]{2,1,0:T(4,128)(2,1)S(1)} %collective-permute-done.5) | copy-start | bytes 245764
  19.9 13.0 %collective-permute-start.6 = (bf16[8,88,4]{2,1,0:T(8,128)(2,1)S(1)}, bf16[8,88,4]{2,1,0:T(8,128)(2,1)S(1)}, u32[]{:S(2)}, u32[]{:S(2)}) collective-permute-start(bf16[8,88,4]{2,1,0:T(8,128)(2,1)S(1)} %get-tuple-element.17), channel_id=1, source_target_pairs={{0,1},{1,0},{2,3},{3,2},{4,5},{5,4},{6,7},{7,6},{8,9},{9,8},{10,11... | collective-permute-start | bytes 16904 | tf_op jit(solution)/shard_map/ppermute | solution.py:33
  21.9 14.1 %collective-permute-start.7 = (bf16[8,88,4]{2,1,0:T(8,128)(2,1)S(1)}, bf16[8,88,4]{2,1,0:T(8,128)(2,1)S(1)}, u32[]{:S(2)}, u32[]{:S(2)}) collective-permute-start(bf16[8,88,4]{2,1,0:T(8,128)(2,1)S(1)} %get-tuple-element.18), channel_id=1, source_target_pairs={{1,0},{0,1},{3,2},{2,3},{5,4},{4,5},{7,6},{6,7},{9,8},{8,9},{11,10... | collective-permute-start | bytes 16904 | tf_op jit(solution)/shard_map/ppermute | solution.py:36
  22.0 5.1 copy-start.6
  22.9 166.7 %collective-permute-start.10 = (bf16[8,88,4]{2,1,0:T(8,128)(2,1)}, bf16[8,88,4]{2,1,0:T(8,128)(2,1)}, u32[]{:S(2)}, u32[]{:S(2)}) collective-permute-start(bf16[8,88,4]{2,1,0:T(8,128)(2,1)} %get-tuple-element.21), channel_id=1, source_target_pairs={{0,1},{1,0},{2,3},{3,2},{4,5},{5,4},{6,7},{7,6},{8,9},{9,8},{10,11... | collective-permute-start | bytes 16904 | tf_op jit(solution)/shard_map/ppermute | solution.py:33
  25.2 164.4 %collective-permute-start.11 = (bf16[8,88,4]{2,1,0:T(8,128)(2,1)}, bf16[8,88,4]{2,1,0:T(8,128)(2,1)}, u32[]{:S(2)}, u32[]{:S(2)}) collective-permute-start(bf16[8,88,4]{2,1,0:T(8,128)(2,1)} %get-tuple-element.22), channel_id=1, source_target_pairs={{1,0},{0,1},{3,2},{2,3},{5,4},{4,5},{7,6},{6,7},{9,8},{8,9},{11,10... | collective-permute-start | bytes 16904 | tf_op jit(solution)/shard_map/ppermute | solution.py:36
  31.4 6.9 copy-start
  113.5 76.2 %copy-start.7 = (bf16[8,4,1280]{2,1,0:T(4,128)(2,1)S(1)}, bf16[8,4,1280]{2,1,0:T(4,128)(2,1)}, u32[]{:S(2)}) copy-start(bf16[8,4,1280]{2,1,0:T(4,128)(2,1)} %copy-done.6) | copy-start | bytes 245764
  189.6 4.3 copy-start.1
  274.5 53.4 %all-to-all-start = ((bf16[24,80,1280]{2,1,0:T(8,128)(2,1)}), bf16[24,80,1280]{2,1,0:T(8,128)(2,1)}, u32[]{:S(2)}, u32[]{:S(2)}) async-start(bf16[24,80,1280]{2,1,0:T(8,128)(2,1)} %bitcast.80), calls=%async_computation | async-start | bytes 9830400 | tf_op jit(solution)/shard_map/all_to_all | solution.py:115
  405.0 6.3 copy-start.9
  405.0 53.7 %all-to-all-start.1 = ((bf16[16,2,38400]{2,1,0:T(2,128)(2,1)}), bf16[16,2,38400]{2,1,0:T(2,128)(2,1)S(1)}, u32[]{:S(2)}, u32[]{:S(2)}) async-start(bf16[16,2,38400]{2,1,0:T(2,128)(2,1)} %reshape.160), calls=%async_computation.1 | async-start | bytes 4915200 | tf_op jit(solution)/shard_map/all_to_all | solution.py:122
  649.5 56.2 %collective-permute-start.12 = (bf16[12,1280,80]{1,2,0:T(8,128)(2,1)S(1)}, bf16[12,1280,80]{1,2,0:T(8,128)(2,1)}, u32[]{:S(2)}, u32[]{:S(2)}) collective-permute-start(bf16[12,1280,80]{1,2,0:T(8,128)(2,1)S(1)} %all_to_all.50), channel_id=1, source_target_pairs={{0,1},{1,0},{2,3},{3,2},{4,5},{5,4},{6,7},{7,6},{8,9},{9,8},{10,11... | collective-permute-start | bytes 7372808 | tf_op jit(solution)/shard_map/ppermute | solution.py:19
